TPU v7x, 256 devices: a whole 4x4x8 slice. The times are simulated.
256 devices in a mesh: seq: 128 (over y, z, x), head: 2 (over core).
Axes of the slice: x: 4, y: 4, z: 8, core: 2. Of those that a mesh axis runs over, the one named last changes fastest.
Arguments:
- queries: bfloat16 [8192, 1536], P('seq', 'head'), may hold values from -6 to 6
- key_vectors: bfloat16 [8192, 512], P('seq', 'head'), may hold values from -6 to 6
- value_vectors: bfloat16 [8192, 512], P('seq', 'head'), may hold values from -6 to 6
- lengths: int32 [64], replicated, may hold values from 1 to 256, 8192 in all
- out_weight: bfloat16 [1536, 1536], P('head', 'seq'), may hold values from -0.15625 to 0.15625
- residual: bfloat16 [8192, 1536], P(('seq', 'head')), may hold values from -6 to 6
- norm_gain: float32 [1536], replicated, may hold values from 0.1 to 1.9
- route_ids: int32 [8192, 6], P(('seq', 'head')), may hold values from 0 to 63, all different within a row; in each aligned block of 32 rows (0 to 31, 32 to 63, ...) at most 6 rows name the same one
- route_logits: float32 [8192, 6], P(('seq', 'head')), may hold values from -8 to 340
- shared_gate_up: bfloat16 [1536, 2, 1024], P(None, None, ('seq', 'head')), may hold values from -0.15625 to 0.15625
- shared_down: bfloat16 [1024, 1536], P(('seq', 'head')), may hold values from -0.1875 to 0.1875
- expert_gate_up: bfloat16 [128, 1536, 2, 256], P('seq'), may hold values from -0.15625 to 0.15625
- expert_down: bfloat16 [128, 256, 1536], P('seq'), may hold values from -0.25 to 0.25
- cache_blocks: bfloat16 [128, 128, 8, 4, 128], P('seq', None, None, 'head'), may hold values from -6 to 6
- block_table: int32 [128], replicated, may hold values from 0 to 127, each once
Outputs:
- layer_out: bfloat16 [8192, 1536], P(('seq', 'head'))
- cache_out: bfloat16 [128, 128, 8, 4, 128], P(None, 'seq', None, 'head')
Inputs may be any that keep to these rules, and one draw needn't show every extreme that they name: The lengths sum to 8192. `route_ids`: each token names 6 different experts; among the tokens of one device no expert is named more than 6 times. `block_table`: every block appears once.
All inputs are finite; a program needn't handle non-finite values.
Results may differ from a plain program's by a relative error of at most 0.0095.
Values may be sent and summed in bfloat16 or wider, within the bound.
A program may use at most 64 MiB of HBM per device.

v0:
```python
import math
import jax
import jax.numpy as jnp
from jax import lax
from jax.sharding import PartitionSpec as P

HD = 128
EXPERTS = 64
TOP = 6
REACH = 4
HALVES = 128
CAP = 6
NEGATIVE = -1e30
EPSILON = 1e-05


def from_behind(shard, axis, by):
    devices = lax.axis_size(axis)
    pairs = [(i, i + by) for i in range(devices) if 0 <= i + by < devices]
    return lax.ppermute(shard, axis, pairs)


def segment_of(positions, lengths):
    request_ends = jnp.cumsum(lengths)
    passed = (request_ends[None, :] <= positions[:, None]).astype(jnp.int32)
    return jnp.sum(passed, axis=1)


def shared_ffn(rows_in, gate_up_part, down_part):
    shared_both = jnp.einsum(
        "td,dcf->tcf", rows_in, gate_up_part, preferred_element_type=jnp.float32
    )
    shared_act = (jax.nn.silu(shared_both[:, 0]) * shared_both[:, 1]).astype(jnp.bfloat16)
    return jnp.dot(shared_act, down_part, preferred_element_type=jnp.float32)


def shards(
    queries,
    key_vectors,
    value_vectors,
    lengths,
    out_weight,
    residual,
    norm_gain,
    route_ids,
    route_logits,
    shared_gate_up,
    shared_down,
    expert_gate_up,
    expert_down,
    cache_blocks,
    block_table,
):
    handed = lax.all_to_all(cache_blocks, "seq", split_axis=1, concat_axis=0, tiled=True)
    cache_out = jnp.take(handed, block_table, axis=0)
    tok_rows = queries.shape[0]
    seq_index = lax.axis_index("seq")
    earlier = [
        from_behind((key_vectors, value_vectors), "seq", offset) for offset in range(REACH, 0, -1)
    ]
    window_keys = jnp.concatenate([member[0] for member in earlier] + [key_vectors], axis=0)
    window_values = jnp.concatenate([member[1] for member in earlier] + [value_vectors], axis=0)
    key_count = window_keys.shape[0]
    kv_heads = key_vectors.shape[1] // HD
    query_heads = queries.shape[1] // HD
    group_size = query_heads // kv_heads
    query_pos = seq_index * tok_rows + jnp.arange(tok_rows, dtype=jnp.int32)
    key_pos = (seq_index - REACH) * tok_rows + jnp.arange(key_count, dtype=jnp.int32)
    visible = (key_pos[None, :] >= 0) & (key_pos[None, :] <= query_pos[:, None])
    visible = visible & (
        segment_of(key_pos, lengths)[None, :] == segment_of(query_pos, lengths)[:, None]
    )
    query_part = queries.reshape(tok_rows, kv_heads, group_size, HD)
    key_part = window_keys.reshape(key_count, kv_heads, HD)
    value_part = window_values.reshape(key_count, kv_heads, HD)
    scores = jnp.einsum(
        "tkgd,wkd->kgtw", query_part, key_part, preferred_element_type=jnp.float32
    ) * (1.0 / math.sqrt(HD))
    scores = jnp.where(visible[None, None], scores, NEGATIVE)
    row_max = jnp.max(scores, axis=-1, keepdims=True)
    weights = jnp.exp(scores - row_max)
    row_total = jnp.sum(weights, axis=-1)
    weighted = jnp.einsum(
        "kgtw,wkd->tkgd",
        weights.astype(jnp.bfloat16),
        value_part,
        preferred_element_type=jnp.float32,
    )
    heads = (weighted / jnp.transpose(row_total, (2, 0, 1))[..., None]).astype(jnp.bfloat16)
    heads = heads.reshape(tok_rows, query_heads * HD)
    partial_out = jnp.dot(
        heads,
        lax.all_gather(out_weight, "seq", axis=1, tiled=True),
        preferred_element_type=jnp.float32,
    )
    attn_out = lax.psum_scatter(partial_out, "head", scatter_dimension=0, tiled=True)
    mixed = residual.astype(jnp.float32) + attn_out
    mean_square = jnp.mean(mixed * mixed, axis=-1, keepdims=True)
    normed = (mixed * lax.rsqrt(mean_square + EPSILON) * norm_gain).astype(jnp.bfloat16)
    gate_up_all, down_all = (
        lax.all_gather(shared_gate_up, ("seq", "head"), axis=2, tiled=True),
        lax.all_gather(shared_down, ("seq", "head"), axis=0, tiled=True),
    )
    shared_part = shared_ffn(normed, gate_up_all, down_all)
    own_tokens = normed.shape[0]
    width_model = normed.shape[1]
    flat_ids = route_ids.reshape(-1)
    onehot = (flat_ids[:, None] == jnp.arange(EXPERTS, dtype=jnp.int32)[None, :]).astype(jnp.int32)
    slot_rank = jnp.sum((jnp.cumsum(onehot, axis=0) - 1) * onehot, axis=1)
    first_slot = flat_ids * CAP + slot_rank
    second_slot = (flat_ids + EXPERTS) * CAP + slot_rank
    token_of = jnp.arange(flat_ids.shape[0], dtype=jnp.int32) // TOP
    routed_rows = normed[token_of]
    outgoing = jnp.zeros((HALVES * CAP, width_model), jnp.bfloat16)
    outgoing = outgoing.at[jnp.concatenate([first_slot, second_slot])].set(
        jnp.concatenate([routed_rows, routed_rows], axis=0)
    )
    local_halves = expert_gate_up.shape[0]
    outgoing = outgoing.reshape(HALVES // local_halves, local_halves, CAP, width_model)
    gate_up = jnp.einsum(
        "nsjd,sdcf->nsjcf",
        lax.all_to_all(outgoing, "seq", split_axis=0, concat_axis=0, tiled=True),
        expert_gate_up,
        preferred_element_type=jnp.float32,
    )
    expert_act = (jax.nn.silu(gate_up[:, :, :, 0]) * gate_up[:, :, :, 1]).astype(jnp.bfloat16)
    half_out = jnp.einsum(
        "nsjf,sfd->nsjd", expert_act, expert_down, preferred_element_type=jnp.float32
    ).astype(jnp.bfloat16)
    returned = lax.all_to_all(half_out, "seq", split_axis=0, concat_axis=0, tiled=True)
    returned = returned.reshape(HALVES * CAP, width_model)
    pair_sum = returned[first_slot].astype(jnp.float32) + returned[second_slot].astype(jnp.float32)
    route_probs = jax.nn.softmax(route_logits, axis=-1)
    routed = jnp.sum(
        route_probs[:, :, None] * pair_sum.reshape(own_tokens, TOP, width_model), axis=1
    )
    layer_out = (mixed + shared_part + routed).astype(jnp.bfloat16)
    return (layer_out, cache_out)


def solution(mesh):
    in_specs = (
        P("seq", "head"),
        P("seq", "head"),
        P("seq", "head"),
        P(),
        P("head", "seq"),
        P(("seq", "head"), None),
        P(),
        P(("seq", "head"), None),
        P(("seq", "head"), None),
        P(None, None, ("seq", "head")),
        P(("seq", "head"), None),
        P("seq", None, None, None),
        P("seq", None, None),
        P("seq", None, None, "head", None),
        P(),
    )
    out_specs = (P(("seq", "head"), None), P(None, "seq", None, "head", None))
    return jax.shard_map(shards, mesh=mesh, in_specs=in_specs, out_specs=out_specs, check_vma=False)
```

profile of v0, /device:TPU:1, one launch (start us, length us, event | category | flops | bytes accessed | tf_op | source)
XLA Modules:
  0.0 410.7 jit_solution(4338545764262982124)
XLA Ops:
  8.1 0.7 all-gather.8.cloned.1.call-update
  8.8 4.4 %collective-permute-start.4 = (bf16[64,256]{1,0:T(8,128)(2,1)}, bf16[64,256]{1,0:T(8,128)(2,1)S(1)}, u32[]{:S(2)}, u32[]{:S(2)}) collective-permute-start(bf16[64,256]{1,0:T(8,128)(2,1)} %param.16), channel_id=1, source_target_pairs={{0,8},{2,10},{4,12},{6,14},{8,16},{10,18},{12,20},{14,22},{16,24},... | collective-permute-start | bytes 98312 | tf_op jit(solution)/shard_map/ppermute | solution.py:20
  13.2 4.4 %collective-permute-start.5 = (bf16[64,256]{1,0:T(8,128)(2,1)}, bf16[64,256]{1,0:T(8,128)(2,1)S(1)}, u32[]{:S(2)}, u32[]{:S(2)}) collective-permute-start(bf16[64,256]{1,0:T(8,128)(2,1)} %param.16), channel_id=1, source_target_pairs={{0,6},{2,8},{4,10},{6,12},{8,14},{10,16},{12,18},{14,20},{16,22},{... | collective-permute-start | bytes 98312 | tf_op jit(solution)/shard_map/ppermute | solution.py:20
  17.6 3.8 collective-permute-start.6
  21.4 2.5 collective-permute-start.7
  23.9 3.6 collective-permute-start
  27.4 0.7 copy.54
  28.2 0.1 reduce-window.18
  28.3 0.1 reduce
  28.4 0.2 convert_reduce_fusion.1
  28.6 0.1 convert_reduce_fusion
  28.7 0.1 compare_and_fusion
  28.8 0.9 reshape.398
  29.8 6.5 %collective-permute-start.1 = (bf16[64,256]{1,0:T(8,128)(2,1)}, bf16[64,256]{1,0:T(8,128)(2,1)S(1)}, u32[]{:S(2)}, u32[]{:S(2)}) collective-permute-start(bf16[64,256]{1,0:T(8,128)(2,1)} %param.17), channel_id=1, source_target_pairs={{0,6},{2,8},{4,10},{6,12},{8,14},{10,16},{12,18},{14,20},{16,22},{... | collective-permute-start | bytes 98312 | tf_op jit(solution)/shard_map/ppermute | solution.py:20
  36.4 3.1 collective-permute-start.2
  39.5 1.4 collective-permute-start.3
  40.9 0.8 constant_dynamic-update-slice_fusion.5
  41.8 0.4 collective-permute-done.3
  42.2 0.8 constant_dynamic-update-slice_fusion
  43.0 0.3 fusion.48
  43.4 0.2 fusion.27
  43.6 0.3 fusion.23
  43.9 0.1 copy.58
  44.1 83.4 %all-gather.8.cloned.1.call-done = bf16[128,12,768]{2,1,0:T(8,128)(2,1)} async-done(((bf16[1,12,768]{2,1,0:T(8,128)(2,1)}), bf16[128,12,768]{2,1,0:T(8,128)(2,1)}) %all-gather.8.cloned.1.call-update) | async-done | bytes 2359312 | tf_op jit(solution)/shard_map/all_gather | solution.py:93
  127.5 3.6 reshape.454
  131.2 1.6 fusion.49
  132.8 0.5 all-gather.10.cloned.1.call-update
  133.4 0.6 copy.59
  134.1 0.1 copy.62
  134.2 0.1 reshape.400
  134.3 0.6 reduce-window.19
  134.9 0.2 slice_reduce_fusion
  135.2 0.1 bitcast_bitcast_fusion
  135.3 0.1 fusion.45
  135.4 12.7 %reduce-scatter.2.cloned.1.call-done = f32[32,1536]{1,0:T(8,128)} async-done(((f32[64,1536]{1,0:T(8,128)}), f32[32,1536]{1,0:T(8,128)}) %reduce-scatter.2.cloned.1.call-update) | async-done | bytes 196624 | tf_op jit(solution)/shard_map/reduce_scatter | solution.py:96
  148.1 1.1 multiply_reduce_fusion.1
  149.2 1.0 multiply_convert_fusion
  150.2 1.9 gather_fusion
  152.1 3.9 scatter_custom_fusion
  156.0 2.5 reshape.403
  158.5 89.1 %all_to_all.22 = bf16[128,1,6,1536]{3,2,1,0:T(8,128)(2,1)} all-to-all(bf16[128,1,6,1536]{3,2,1,0:T(8,128)(2,1)} %bitcast.96), channel_id=1, replica_groups=mesh['seq'=128,'head'=2] {'seq'}, dimensions={0} | all-to-all | bytes 4718592 | tf_op jit(solution)/shard_map/all_to_all | solution.py:122
  247.6 10.7 %all-to-all-start.2 = ((bf16[1,128,8,2,128]{4,3,2,0,1:T(2,128)(2,1)}), bf16[1,128,8,2,128]{4,3,2,0,1:T(2,128)(2,1)S(1)}, u32[]{:S(2)}, u32[]{:S(2)}) async-start(bf16[1,128,8,2,128]{4,3,2,0,1:T(2,128)(2,1)} %bitcast.36), calls=%async_computation.3 | async-start | bytes 1048576 | tf_op jit(solution)/shard_map/all_to_all | solution.py:54
  258.3 3.3 fusion.10
  261.6 0.8 fusion.2
  262.4 3.0 copy.68
  265.3 9.3 %all-to-all-done.2 = bf16[1,128,8,2,128]{4,3,2,0,1:T(2,128)(2,1)S(1)} async-done(((bf16[1,128,8,2,128]{4,3,2,0,1:T(2,128)(2,1)}), bf16[1,128,8,2,128]{4,3,2,0,1:T(2,128)(2,1)S(1)}, u32[]{:S(2)}, u32[]{:S(2)}) %all-to-all-start.2) | async-done | bytes 524320 | tf_op jit(solution)/shard_map/all_to_all | solution.py:54
  274.6 8.9 %all-to-all-start.1 = ((bf16[128,1,6,1536]{3,2,1,0:T(8,128)(2,1)}), bf16[128,1,6,1536]{3,2,1,0:T(8,128)(2,1)}, u32[]{:S(2)}, u32[]{:S(2)}) async-start(bf16[128,1,6,1536]{3,2,1,0:T(8,128)(2,1)} %copy.68), calls=%async_computation.2 | async-start | bytes 6291456 | tf_op jit(solution)/shard_map/all_to_all | solution.py:130
  283.6 0.1 copy.69
  283.7 0.1 mul.140
  283.8 0.1 copy.70
  283.9 0.1 mul.142
  284.0 0.1 copy.61
  284.2 1.6 gather_fusion.3
  285.8 1.4 fusion.26
  287.2 5.9 %reshape.456 = bf16[1024,1536]{1,0:T(8,128)(2,1)} reshape(bf16[256,4,1536]{2,1,0:T(4,128)(2,1)} %all-gather.10.cloned.1.call-done) | data formatting | bytes 6291456
  293.1 91.6 %all-gather.6.cloned.1.call-done = bf16[1536,2,1024]{0,1,2:T(2,128)(2,1)} async-done(((bf16[1536,2,4]{0,1,2:T(2,128)(2,1)}), bf16[1536,2,1024]{0,1,2:T(2,128)(2,1)}) %all-gather.6.cloned.1.call-update) | async-done | bytes 6291472 | tf_op jit(solution)/shard_map/all_gather | solution.py:101
  384.8 5.5 %fusion = f32[32,2,1024]{2,0,1:T(8,128)} fusion(bf16[1536,2,1024]{0,1,2:T(2,128)(2,1)} %all-gather.6.cloned.1.call-done, bf16[32,1536]{1,0:T(8,128)(2,1)S(1)} %multiply_convert_fusion), kind=kOutput, calls=%fused_computation.5 | convolution fusion | flops 201326592 | bytes 6651904 | tf_op jit(solution)/shard_map/td,dcf->tcf/dot_general | solution.py:30
  390.2 3.7 reshape.407
  393.9 1.9 gather_fusion.1
  395.8 1.9 gather_fusion.2
  397.7 1.4 convert_add_fusion
  399.1 0.2 add.235
  399.3 0.6 multiply_reduce_fusion
  399.8 3.4 fusion.7
  (63 shorter events, 0.7 us)
Async XLA Ops:
  8.0 253.6 %copy-start = (bf16[1,256,1536]{2,1,0:T(8,128)(2,1)S(1)}, bf16[1,256,1536]{2,1,0:T(8,128)(2,1)}, u32[]{:S(2)}) copy-start(bf16[1,256,1536]{2,1,0:T(8,128)(2,1)} %param.27) | copy-start | bytes 2359300
  8.0 119.5 %all-gather.8.cloned.1.call-start = ((), (), s32[]{:S(2)}) async-start(), calls=%async_computation.6 | async-start | bytes 3170304 | tf_op jit(solution)/shard_map/all_gather | solution.py:93
  8.7 139.4 %reduce-scatter.2.cloned.1.call-start = ((), (), s32[]{:S(2)}) async-start(), calls=%async_computation.4 | async-start | bytes 589824 | tf_op jit(solution)/shard_map/reduce_scatter | solution.py:96
  8.8 21.0 %collective-permute-start.4 = (bf16[64,256]{1,0:T(8,128)(2,1)}, bf16[64,256]{1,0:T(8,128)(2,1)S(1)}, u32[]{:S(2)}, u32[]{:S(2)}) collective-permute-start(bf16[64,256]{1,0:T(8,128)(2,1)} %param.16), channel_id=1, source_target_pairs={{0,8},{2,10},{4,12},{6,14},{8,16},{10,18},{12,20},{14,22},{16,24},... | collective-permute-start | bytes 98312 | tf_op jit(solution)/shard_map/ppermute | solution.py:20
  13.2 23.2 %collective-permute-start.5 = (bf16[64,256]{1,0:T(8,128)(2,1)}, bf16[64,256]{1,0:T(8,128)(2,1)S(1)}, u32[]{:S(2)}, u32[]{:S(2)}) collective-permute-start(bf16[64,256]{1,0:T(8,128)(2,1)} %param.16), channel_id=1, source_target_pairs={{0,6},{2,8},{4,10},{6,12},{8,14},{10,16},{12,18},{14,20},{16,22},{... | collective-permute-start | bytes 98312 | tf_op jit(solution)/shard_map/ppermute | solution.py:20
  17.6 22.0 %collective-permute-start.6 = (bf16[64,256]{1,0:T(8,128)(2,1)}, bf16[64,256]{1,0:T(8,128)(2,1)S(1)}, u32[]{:S(2)}, u32[]{:S(2)}) collective-permute-start(bf16[64,256]{1,0:T(8,128)(2,1)} %param.16), channel_id=1, source_target_pairs={{0,4},{2,6},{4,8},{6,10},{8,12},{10,14},{12,16},{14,18},{16,20},{1... | collective-permute-start | bytes 98312 | tf_op jit(solution)/shard_map/ppermute | solution.py:20
  21.4 19.5 %collective-permute-start.7 = (bf16[64,256]{1,0:T(8,128)(2,1)}, bf16[64,256]{1,0:T(8,128)(2,1)S(1)}, u32[]{:S(2)}, u32[]{:S(2)}) collective-permute-start(bf16[64,256]{1,0:T(8,128)(2,1)} %param.16), channel_id=1, source_target_pairs={{0,2},{2,4},{4,6},{6,8},{8,10},{10,12},{12,14},{14,16},{16,18},{18... | collective-permute-start | bytes 98312 | tf_op jit(solution)/shard_map/ppermute | solution.py:20
  23.9 17.8 %collective-permute-start = (bf16[64,256]{1,0:T(8,128)(2,1)}, bf16[64,256]{1,0:T(8,128)(2,1)S(1)}, u32[]{:S(2)}, u32[]{:S(2)}) collective-permute-start(bf16[64,256]{1,0:T(8,128)(2,1)} %param.17), channel_id=1, source_target_pairs={{0,8},{2,10},{4,12},{6,14},{8,16},{10,18},{12,20},{14,22},{16,24},... | collective-permute-start | bytes 98312 | tf_op jit(solution)/shard_map/ppermute | solution.py:20
  29.8 11.9 %collective-permute-start.1 = (bf16[64,256]{1,0:T(8,128)(2,1)}, bf16[64,256]{1,0:T(8,128)(2,1)S(1)}, u32[]{:S(2)}, u32[]{:S(2)}) collective-permute-start(bf16[64,256]{1,0:T(8,128)(2,1)} %param.17), channel_id=1, source_target_pairs={{0,6},{2,8},{4,10},{6,12},{8,14},{10,16},{12,18},{14,20},{16,22},{... | collective-permute-start | bytes 98312 | tf_op jit(solution)/shard_map/ppermute | solution.py:20
  36.4 5.4 %collective-permute-start.2 = (bf16[64,256]{1,0:T(8,128)(2,1)}, bf16[64,256]{1,0:T(8,128)(2,1)S(1)}, u32[]{:S(2)}, u32[]{:S(2)}) collective-permute-start(bf16[64,256]{1,0:T(8,128)(2,1)} %param.17), channel_id=1, source_target_pairs={{0,4},{2,6},{4,8},{6,10},{8,12},{10,14},{12,16},{14,18},{16,20},{1... | collective-permute-start | bytes 98312 | tf_op jit(solution)/shard_map/ppermute | solution.py:20
  39.5 2.7 collective-permute-start.3
  131.1 2.3 copy-start.3
  131.1 2.9 copy-start.4
  131.2 16.9 %copy-start.1 = (bf16[32,1536]{1,0:T(8,128)(2,1)S(1)}, bf16[32,1536]{1,0:T(8,128)(2,1)}, u32[]{:S(2)}) copy-start(bf16[32,1536]{1,0:T(8,128)(2,1)} %param.20) | copy-start | bytes 294916
  131.2 18.0 %copy-start.5 = (f32[1536]{0:T(1024)S(1)}, f32[1536]{0:T(1024)}, u32[]{:S(2)}) copy-start(f32[1536]{0:T(1024)} %param.21) | copy-start | bytes 18436
  132.8 154.4 %all-gather.10.cloned.1.call-start = ((), (), s32[]{:S(2)}) async-start(), calls=%async_computation.7 | async-start | bytes 3158016 | tf_op jit(solution)/shard_map/all_gather | solution.py:102
  133.4 251.4 %all-gather.6.cloned.1.call-start = ((), (), s32[]{:S(2)}) async-start(), calls=%async_computation.5 | async-start | bytes 6316032 | tf_op jit(solution)/shard_map/all_gather | solution.py:101
  158.5 99.8 %copy-start.6 = (bf16[1,1536,2,256]{3,2,1,0:T(2,128)(2,1)S(1)}, bf16[1,1536,2,256]{3,2,1,0:T(2,128)(2,1)}, u32[]{:S(2)}) copy-start(bf16[1,1536,2,256]{3,2,1,0:T(2,128)(2,1)} %param.26) | copy-start | bytes 4718596
  247.6 27.1 %all-to-all-start.2 = ((bf16[1,128,8,2,128]{4,3,2,0,1:T(2,128)(2,1)}), bf16[1,128,8,2,128]{4,3,2,0,1:T(2,128)(2,1)S(1)}, u32[]{:S(2)}, u32[]{:S(2)}) async-start(bf16[1,128,8,2,128]{4,3,2,0,1:T(2,128)(2,1)} %bitcast.36), calls=%async_computation.3 | async-start | bytes 1048576 | tf_op jit(solution)/shard_map/all_to_all | solution.py:54
  265.3 18.6 %copy-start.2 = (f32[32,6]{0,1:T(8,128)S(1)}, f32[32,6]{0,1:T(8,128)}, u32[]{:S(2)}) copy-start(f32[32,6]{0,1:T(8,128)} %param.23) | copy-start | bytes 2308
  265.3 18.8 %copy-start.7 = (s32[128]{0:T(128)S(1)}, s32[128]{0:T(128)}, u32[]{:S(2)}) copy-start(s32[128]{0:T(128)} %param.29) | copy-start | bytes 1540
  274.6 115.6 %all-to-all-start.1 = ((bf16[128,1,6,1536]{3,2,1,0:T(8,128)(2,1)}), bf16[128,1,6,1536]{3,2,1,0:T(8,128)(2,1)}, u32[]{:S(2)}, u32[]{:S(2)}) async-start(bf16[128,1,6,1536]{3,2,1,0:T(8,128)(2,1)} %copy.68), calls=%async_computation.2 | async-start | bytes 6291456 | tf_op jit(solution)/shard_map/all_to_all | solution.py:130
Sparse Core Ops, SparseCore 0:
  12.5 114.9 all-gather.7
  132.9 15.1 reduce-scatter.1
Sparse Core Ops, SparseCore 1:
  137.6 121.0 all-gather.9
  263.6 121.1 all-gather.5
where the time goes:
time: 412 us; the launch traced here: 411 us
  waiting for transfers between devices  199 us (48%)
  blocking collectives  89.1 us (22%)
  starting transfers between devices  49.4 us (12%)
  local copies, waits for them, and re-layouts  31.2 us (8%)
  between operations  16 us (4%)
  matrix products  15.2 us (4%)
  other arithmetic  11.1 us (3%)
    all_gather x1, waiting for transfers between devices, shards(): lax.all_gather(shared_gate_up, ('seq', 'head'), axis=2, tiled=True)  91.6 us
    all_to_all x1, blocking collectives, shards(): lax.all_to_all(outgoing, 'seq', split_axis=0, concat_axis=0, tiled=True)  89.1 us
    all_gather x1, waiting for transfers between devices, shards(): lax.all_gather(out_weight, 'seq', axis=1, tiled=True)  83.4 us
    ppermute x8, starting transfers between devices, from_behind(): return lax.ppermute(shard, axis, pairs)  29.7 us
    reduce_scatter x1, waiting for transfers between devices, shards(): lax.psum_scatter(partial_out, 'head', scatter_dimension=0, tiled=True)  12.7 us
    all_to_all x1, starting transfers between devices, shards(): lax.all_to_all(cache_blocks, 'seq', split_axis=1, concat_axis=0, tiled=True)  10.7 us
    unnamed x28, local copies, waits for them, and re-layouts  10.3 us
    all_to_all x1, waiting for transfers between devices, shards(): lax.all_to_all(cache_blocks, 'seq', split_axis=1, concat_axis=0, tiled=True)  9.29 us
  transfers between devices with their start and end apart: 14, of which 5 were waited for; matrix products, arithmetic and copies ran while one was open for 10% of the time, Pallas kernels for 0%

commit v1 on v0

--- a/solution.py
+++ b/solution.py
@@ -51,7 +51,12 @@
     cache_blocks,
     block_table,
 ):
-    handed = lax.all_to_all(cache_blocks, "seq", split_axis=1, concat_axis=0, tiled=True)
+    handed = jnp.concatenate(
+        lax.all_to_all(
+            jnp.stack(jnp.split(cache_blocks, lax.axis_size("seq"), axis=1)), "seq", 0, 0
+        ),
+        axis=0,
+    )
     cache_out = jnp.take(handed, block_table, axis=0)
     tok_rows = queries.shape[0]
     seq_index = lax.axis_index("seq")

time: 412 us -> 504 us (1.22)
  the two profiles are of different devices: /device:TPU:1 before, /device:TPU:32 now
where the time goes in v1:
time: 504 us; the launch traced here: 499 us
  waiting for transfers between devices  204 us (40%)
  local copies, waits for them, and re-layouts  195 us (39%)
  starting transfers between devices  56.9 us (11%)
  between operations  16.1 us (3%)
  matrix products  15.2 us (3%)
  other arithmetic  11.1 us (2%)
    unnamed x155, local copies, waits for them, and re-layouts  173 us
    all_gather x1, waiting for transfers between devices, shards(): lax.all_gather(out_weight, 'seq', axis=1, tiled=True)  79.6 us
    all_to_all x1, waiting for transfers between devices, shards(): lax.all_to_all(outgoing, 'seq', split_axis=0, concat_axis=0, tiled=True)  56.2 us
    all_to_all x1, waiting for transfers between devices, shards(): lax.all_to_all(half_out, 'seq', split_axis=0, concat_axis=0, tiled=True)  54 us
    ppermute x8, starting transfers between devices, from_behind(): return lax.ppermute(shard, axis, pairs)  30.5 us
    all_to_all x1, starting transfers between devices, shards(): lax.all_to_all(outgoing, 'seq', split_axis=0, concat_axis=0, tiled=True)  11.2 us
  transfers between devices with their start and end apart: 15, of which 6 were waited for; matrix products, arithmetic and copies ran while one was open for 41% of the time, Pallas kernels for 0%

profile of v1, /device:TPU:32, one launch (start us, length us, event | category | flops | bytes accessed | tf_op | source)
XLA Modules:
  0.0 498.8 jit_solution(3453965950669839138)
XLA Ops:
  8.8 3.8 collective-permute-start.4
  12.6 4.7 collective-permute-start.5
  17.3 4.1 collective-permute-start.6
  21.4 2.8 collective-permute-start.7
  24.2 5.0 %collective-permute-start = (bf16[64,256]{1,0:T(8,128)(2,1)}, bf16[64,256]{1,0:T(8,128)(2,1)S(1)}, u32[]{:S(2)}, u32[]{:S(2)}) collective-permute-start(bf16[64,256]{1,0:T(8,128)(2,1)} %param.17), channel_id=1, source_target_pairs={{0,8},{2,10},{4,12},{6,14},{8,16},{10,18},{12,20},{14,22},{16,24},... | collective-permute-start | bytes 98312 | tf_op jit(solution)/shard_map/ppermute | solution.py:20
  31.6 4.7 collective-permute-start.1
  36.3 3.4 collective-permute-start.2
  39.8 1.9 collective-permute-start.3
  42.5 2.5 collective-permute-done.2
  45.1 2.8 collective-permute-done.3
  49.8 79.6 %all-gather.8.cloned.1.call-done = bf16[128,12,768]{2,1,0:T(8,128)(2,1)} async-done(((bf16[1,12,768]{2,1,0:T(8,128)(2,1)}), bf16[128,12,768]{2,1,0:T(8,128)(2,1)}) %all-gather.8.cloned.1.call-update) | async-done | bytes 2359312 | tf_op jit(solution)/shard_map/all_gather | solution.py:98
  129.4 3.6 reshape.455
  133.0 1.6 fusion.48
  137.2 1.3 constant_dynamic-update-slice_fusion.137
  138.4 1.3 constant_dynamic-update-slice_fusion.136
  139.7 1.3 constant_dynamic-update-slice_fusion.135
  142.3 1.3 constant_dynamic-update-slice_fusion.133
  143.6 1.3 constant_dynamic-update-slice_fusion.132
  144.9 1.3 constant_dynamic-update-slice_fusion.131
  146.1 1.3 constant_dynamic-update-slice_fusion.130
  147.4 1.3 constant_dynamic-update-slice_fusion.129
  148.7 1.3 constant_dynamic-update-slice_fusion.128
  150.0 1.3 constant_dynamic-update-slice_fusion.127
  151.3 1.3 constant_dynamic-update-slice_fusion.126
  153.8 1.3 constant_dynamic-update-slice_fusion.124
  155.1 1.3 constant_dynamic-update-slice_fusion.123
  157.7 1.3 constant_dynamic-update-slice_fusion.121
  159.0 1.3 constant_dynamic-update-slice_fusion.120
  160.3 1.3 constant_dynamic-update-slice_fusion.119
  161.6 1.3 constant_dynamic-update-slice_fusion.118
  162.8 1.3 constant_dynamic-update-slice_fusion.117
  164.1 1.3 constant_dynamic-update-slice_fusion.116
  165.4 1.3 constant_dynamic-update-slice_fusion.115
  168.0 1.3 constant_dynamic-update-slice_fusion.113
  169.3 1.3 constant_dynamic-update-slice_fusion.112
  170.5 1.3 constant_dynamic-update-slice_fusion.111
  191.1 1.3 constant_dynamic-update-slice_fusion.95
  205.2 1.3 constant_dynamic-update-slice_fusion.84
  221.9 1.3 constant_dynamic-update-slice_fusion.71
  259.1 1.3 constant_dynamic-update-slice_fusion.42
  265.6 1.3 constant_dynamic-update-slice_fusion.37
  276.7 1.9 gather_fusion
  278.6 3.9 scatter_custom_fusion
  282.5 2.5 reshape.403
  285.0 11.2 %all-to-all-start = ((bf16[128,1,6,1536]{3,2,1,0:T(8,128)(2,1)}), bf16[128,1,6,1536]{3,2,1,0:T(8,128)(2,1)}, u32[]{:S(2)}, u32[]{:S(2)}) async-start(bf16[128,1,6,1536]{3,2,1,0:T(8,128)(2,1)} %bitcast.347), calls=%async_computation.1 | async-start | bytes 6291456 | tf_op jit(solution)/shard_map/all_to_all | solution.py:127
  296.3 1.3 constant_dynamic-update-slice_fusion.30
  301.4 1.3 constant_dynamic-update-slice_fusion.26
  321.9 1.3 constant_dynamic-update-slice_fusion.10
  323.2 56.2 %all-to-all-done = bf16[128,1,6,1536]{3,2,1,0:T(8,128)(2,1)} async-done(((bf16[128,1,6,1536]{3,2,1,0:T(8,128)(2,1)}), bf16[128,1,6,1536]{3,2,1,0:T(8,128)(2,1)}, u32[]{:S(2)}, u32[]{:S(2)}) %all-to-all-start) | async-done | bytes 2359328 | tf_op jit(solution)/shard_map/all_to_all | solution.py:127
  379.4 7.3 %all-to-all-start.2 = ((bf16[128,1,1,8,2,128]{5,4,3,2,1,0:T(2,128)(2,1)}), bf16[128,1,1,8,2,128]{5,4,3,2,1,0:T(2,128)(2,1)S(1)}, u32[]{:S(2)}, u32[]{:S(2)}) async-start(bf16[128,1,1,8,2,128]{5,4,3,2,1,0:T(2,128)(2,1)} %constant_dynamic-update-slice_fusion.10), calls=%async_computation.3 | async-start | bytes 1048576 | tf_op jit(solution)/shard_map/all_to_all | solution.py:55
  386.7 3.3 fusion.10
  390.8 3.0 copy.66
  393.8 7.8 %all-to-all-done.2 = bf16[128,1,1,8,2,128]{5,4,3,2,1,0:T(2,128)(2,1)S(1)} async-done(((bf16[128,1,1,8,2,128]{5,4,3,2,1,0:T(2,128)(2,1)}), bf16[128,1,1,8,2,128]{5,4,3,2,1,0:T(2,128)(2,1)S(1)}, u32[]{:S(2)}, u32[]{:S(2)}) %all-to-all-start.2) | async-done | bytes 524320 | tf_op jit(solution)/shard_map/all_to_all | solution.py:55
  401.6 7.8 %all-to-all-start.1 = ((bf16[128,1,6,1536]{3,2,1,0:T(8,128)(2,1)}), bf16[128,1,6,1536]{3,2,1,0:T(8,128)(2,1)}, u32[]{:S(2)}, u32[]{:S(2)}) async-start(bf16[128,1,6,1536]{3,2,1,0:T(8,128)(2,1)} %copy.66), calls=%async_computation.2 | async-start | bytes 6291456 | tf_op jit(solution)/shard_map/all_to_all | solution.py:135
  410.0 1.6 gather_fusion.3
  411.7 1.4 broadcast_select_fusion
  413.0 5.9 %reshape.457 = bf16[1024,1536]{1,0:T(8,128)(2,1)} reshape(bf16[256,4,1536]{2,1,0:T(4,128)(2,1)} %all-gather.10.cloned.1.call-done) | data formatting | bytes 6291456
  418.9 5.5 %fusion = f32[32,2,1024]{2,0,1:T(8,128)} fusion(bf16[1536,2,1024]{0,1,2:T(2,128)(2,1)} %all-gather.6.cloned.1.call-done, bf16[32,1536]{1,0:T(8,128)(2,1)S(1)} %multiply_convert_fusion), kind=kOutput, calls=%fused_computation.5 | convolution fusion | flops 201326592 | bytes 6651904 | tf_op jit(solution)/shard_map/td,dcf->tcf/dot_general | solution.py:30
  424.4 54.0 %all-to-all-done.1 = bf16[128,1,6,1536]{3,2,1,0:T(8,128)(2,1)} async-done(((bf16[128,1,6,1536]{3,2,1,0:T(8,128)(2,1)}), bf16[128,1,6,1536]{3,2,1,0:T(8,128)(2,1)}, u32[]{:S(2)}, u32[]{:S(2)}) %all-to-all-start.1) | async-done | bytes 2359328 | tf_op jit(solution)/shard_map/all_to_all | solution.py:135
  478.4 3.7 reshape.407
  482.1 1.9 gather_fusion.1
  483.9 1.9 gather_fusion.2
  485.8 1.4 convert_add_fusion
  488.0 3.4 fusion.7
  (192 shorter events, 137.0 us)
Async XLA Ops:
  8.0 382.0 %copy-start = (bf16[1,256,1536]{2,1,0:T(8,128)(2,1)S(1)}, bf16[1,256,1536]{2,1,0:T(8,128)(2,1)}, u32[]{:S(2)}) copy-start(bf16[1,256,1536]{2,1,0:T(8,128)(2,1)} %param.27) | copy-start | bytes 2359300
  8.0 121.3 %all-gather.8.cloned.1.call-start = ((), (), s32[]{:S(2)}) async-start(), calls=%async_computation.6 | async-start | bytes 3170304 | tf_op jit(solution)/shard_map/all_gather | solution.py:98
  8.7 265.9 %reduce-scatter.2.cloned.1.call-start = ((), (), s32[]{:S(2)}) async-start(), calls=%async_computation.4 | async-start | bytes 589824 | tf_op jit(solution)/shard_map/reduce_scatter | solution.py:101
  8.8 22.8 %collective-permute-start.4 = (bf16[64,256]{1,0:T(8,128)(2,1)}, bf16[64,256]{1,0:T(8,128)(2,1)S(1)}, u32[]{:S(2)}, u32[]{:S(2)}) collective-permute-start(bf16[64,256]{1,0:T(8,128)(2,1)} %param.16), channel_id=1, source_target_pairs={{0,8},{2,10},{4,12},{6,14},{8,16},{10,18},{12,20},{14,22},{16,24},... | collective-permute-start | bytes 98312 | tf_op jit(solution)/shard_map/ppermute | solution.py:20
  12.6 23.7 %collective-permute-start.5 = (bf16[64,256]{1,0:T(8,128)(2,1)}, bf16[64,256]{1,0:T(8,128)(2,1)S(1)}, u32[]{:S(2)}, u32[]{:S(2)}) collective-permute-start(bf16[64,256]{1,0:T(8,128)(2,1)} %param.16), channel_id=1, source_target_pairs={{0,6},{2,8},{4,10},{6,12},{8,14},{10,16},{12,18},{14,20},{16,22},{... | collective-permute-start | bytes 98312 | tf_op jit(solution)/shard_map/ppermute | solution.py:20
  17.3 22.5 %collective-permute-start.6 = (bf16[64,256]{1,0:T(8,128)(2,1)}, bf16[64,256]{1,0:T(8,128)(2,1)S(1)}, u32[]{:S(2)}, u32[]{:S(2)}) collective-permute-start(bf16[64,256]{1,0:T(8,128)(2,1)} %param.16), channel_id=1, source_target_pairs={{0,4},{2,6},{4,8},{6,10},{8,12},{10,14},{12,16},{14,18},{16,20},{1... | collective-permute-start | bytes 98312 | tf_op jit(solution)/shard_map/ppermute | solution.py:20
  21.4 20.3 %collective-permute-start.7 = (bf16[64,256]{1,0:T(8,128)(2,1)}, bf16[64,256]{1,0:T(8,128)(2,1)S(1)}, u32[]{:S(2)}, u32[]{:S(2)}) collective-permute-start(bf16[64,256]{1,0:T(8,128)(2,1)} %param.16), channel_id=1, source_target_pairs={{0,2},{2,4},{4,6},{6,8},{8,10},{10,12},{12,14},{14,16},{16,18},{18... | collective-permute-start | bytes 98312 | tf_op jit(solution)/shard_map/ppermute | solution.py:20
  24.2 18.3 %collective-permute-start = (bf16[64,256]{1,0:T(8,128)(2,1)}, bf16[64,256]{1,0:T(8,128)(2,1)S(1)}, u32[]{:S(2)}, u32[]{:S(2)}) collective-permute-start(bf16[64,256]{1,0:T(8,128)(2,1)} %param.17), channel_id=1, source_target_pairs={{0,8},{2,10},{4,12},{6,14},{8,16},{10,18},{12,20},{14,22},{16,24},... | collective-permute-start | bytes 98312 | tf_op jit(solution)/shard_map/ppermute | solution.py:20
  31.6 10.9 %collective-permute-start.1 = (bf16[64,256]{1,0:T(8,128)(2,1)}, bf16[64,256]{1,0:T(8,128)(2,1)S(1)}, u32[]{:S(2)}, u32[]{:S(2)}) collective-permute-start(bf16[64,256]{1,0:T(8,128)(2,1)} %param.17), channel_id=1, source_target_pairs={{0,6},{2,8},{4,10},{6,12},{8,14},{10,16},{12,18},{14,20},{16,22},{... | collective-permute-start | bytes 98312 | tf_op jit(solution)/shard_map/ppermute | solution.py:20
  36.3 8.7 %collective-permute-start.2 = (bf16[64,256]{1,0:T(8,128)(2,1)}, bf16[64,256]{1,0:T(8,128)(2,1)S(1)}, u32[]{:S(2)}, u32[]{:S(2)}) collective-permute-start(bf16[64,256]{1,0:T(8,128)(2,1)} %param.17), channel_id=1, source_target_pairs={{0,4},{2,6},{4,8},{6,10},{8,12},{10,14},{12,16},{14,18},{16,20},{1... | collective-permute-start | bytes 98312 | tf_op jit(solution)/shard_map/ppermute | solution.py:20
  39.8 8.1 %collective-permute-start.3 = (bf16[64,256]{1,0:T(8,128)(2,1)}, bf16[64,256]{1,0:T(8,128)(2,1)S(1)}, u32[]{:S(2)}, u32[]{:S(2)}) collective-permute-start(bf16[64,256]{1,0:T(8,128)(2,1)} %param.17), channel_id=1, source_target_pairs={{0,2},{2,4},{4,6},{6,8},{8,10},{10,12},{12,14},{14,16},{16,18},{18... | collective-permute-start | bytes 98312 | tf_op jit(solution)/shard_map/ppermute | solution.py:20
  133.0 2.3 copy-start.3
  133.0 2.9 copy-start.4
  133.0 141.6 %copy-start.1 = (bf16[32,1536]{1,0:T(8,128)(2,1)S(1)}, bf16[32,1536]{1,0:T(8,128)(2,1)}, u32[]{:S(2)}) copy-start(bf16[32,1536]{1,0:T(8,128)(2,1)} %param.20) | copy-start | bytes 294916
  133.0 142.7 %copy-start.5 = (f32[1536]{0:T(1024)S(1)}, f32[1536]{0:T(1024)}, u32[]{:S(2)}) copy-start(f32[1536]{0:T(1024)} %param.21) | copy-start | bytes 18436
  134.6 278.4 %all-gather.10.cloned.1.call-start = ((), (), s32[]{:S(2)}) async-start(), calls=%async_computation.7 | async-start | bytes 3158016 | tf_op jit(solution)/shard_map/all_gather | solution.py:107
  135.2 283.7 %all-gather.6.cloned.1.call-start = ((), (), s32[]{:S(2)}) async-start(), calls=%async_computation.5 | async-start | bytes 6316032 | tf_op jit(solution)/shard_map/all_gather | solution.py:106
  285.0 101.7 %copy-start.6 = (bf16[1,1536,2,256]{3,2,1,0:T(2,128)(2,1)S(1)}, bf16[1,1536,2,256]{3,2,1,0:T(2,128)(2,1)}, u32[]{:S(2)}) copy-start(bf16[1,1536,2,256]{3,2,1,0:T(2,128)(2,1)} %param.26) | copy-start | bytes 4718596
  285.0 94.4 %all-to-all-start = ((bf16[128,1,6,1536]{3,2,1,0:T(8,128)(2,1)}), bf16[128,1,6,1536]{3,2,1,0:T(8,128)(2,1)}, u32[]{:S(2)}, u32[]{:S(2)}) async-start(bf16[128,1,6,1536]{3,2,1,0:T(8,128)(2,1)} %bitcast.347), calls=%async_computation.1 | async-start | bytes 6291456 | tf_op jit(solution)/shard_map/all_to_all | solution.py:127
  379.4 22.2 %all-to-all-start.2 = ((bf16[128,1,1,8,2,128]{5,4,3,2,1,0:T(2,128)(2,1)}), bf16[128,1,1,8,2,128]{5,4,3,2,1,0:T(2,128)(2,1)S(1)}, u32[]{:S(2)}, u32[]{:S(2)}) async-start(bf16[128,1,1,8,2,128]{5,4,3,2,1,0:T(2,128)(2,1)} %constant_dynamic-update-slice_fusion.10), calls=%async_computation.3 | async-start | bytes 1048576 | tf_op jit(solution)/shard_map/all_to_all | solution.py:55
  393.8 16.0 %copy-start.2 = (f32[32,6]{0,1:T(8,128)S(1)}, f32[32,6]{0,1:T(8,128)}, u32[]{:S(2)}) copy-start(f32[32,6]{0,1:T(8,128)} %param.23) | copy-start | bytes 2308
  393.8 16.1 %copy-start.7 = (s32[128]{0:T(128)S(1)}, s32[128]{0:T(128)}, u32[]{:S(2)}) copy-start(s32[128]{0:T(128)} %param.29) | copy-start | bytes 1540
  401.6 76.7 %all-to-all-start.1 = ((bf16[128,1,6,1536]{3,2,1,0:T(8,128)(2,1)}), bf16[128,1,6,1536]{3,2,1,0:T(8,128)(2,1)}, u32[]{:S(2)}, u32[]{:S(2)}) async-start(bf16[128,1,6,1536]{3,2,1,0:T(8,128)(2,1)} %copy.66), calls=%async_computation.2 | async-start | bytes 6291456 | tf_op jit(solution)/shard_map/all_to_all | solution.py:135
Sparse Core Ops, SparseCore 0:
  12.5 116.7 all-gather.7
  134.8 11.3 reduce-scatter.1
Sparse Core Ops, SparseCore 1:
  139.5 103.6 all-gather.9
  248.1 127.8 all-gather.5
